TPU v7x, 128 devices: a whole 4x4x4 slice. The times are simulated.
128 devices in a mesh: seq: 4 (over y_hi, core), fsdp: 32 (over z, x, y_lo).
Axes of the slice: x: 4, y: 4 (y_hi: 2, y_lo: 2; y = y_hi * 2 + y_lo), z: 4, core: 2. Of those that a mesh axis runs over, the one named last changes fastest.
Arguments:
- hidden_in: bfloat16 [2048, 16384], P('seq', 'fsdp'), may hold values from -6 to 6
- gain_in: float32 [16384], P('fsdp'), may hold values from 0.25 to 1.75
- w_query: bfloat16 [16384, 4096], P('fsdp'), may hold values from -0.046875 to 0.046875
- query_scale: float32 [4096], replicated, may hold values from 0.5 to 2
- w_key: bfloat16 [16384, 256], P('fsdp'), may hold values from -0.046875 to 0.046875
- key_scale: float32 [256], replicated, may hold values from 0.5 to 2
- w_value: bfloat16 [16384, 256], P('fsdp'), may hold values from -0.046875 to 0.046875
- value_scale: float32 [256], replicated, may hold values from 0.5 to 2
- w_out: bfloat16 [4096, 16384], P(None, 'fsdp'), may hold values from -0.125 to 0.125
- out_scale: float32 [16384], P('fsdp'), may hold values from 0.5 to 2
- gain_mid: float32 [16384], P('fsdp'), may hold values from 0.25 to 1.75
- head_order: int32 [32], replicated, may hold values from 0 to 31, each once
Outputs:
- hessian: float32 [16384, 16384], P('fsdp', 'seq')
- residual_out: bfloat16 [2048, 16384], P('seq', 'fsdp')
All inputs are finite; a program needn't handle non-finite values.
Results may differ from a plain program's by a relative error of at most 0.009.
Values may be sent and summed in bfloat16 or wider, within the bound.
No kernel may reach another device: no remote copies, remote signals or barrier semaphores. Data moves between devices by JAX's collectives and lax.ppermute only.
A program may use at most 128 MiB of HBM per device.

v0:
```python
import jax
import jax.numpy as jnp
import numpy as np
from jax import lax
from jax.experimental import pallas as pl
from jax.experimental.pallas import tpu as pltpu
from jax.sharding import Mesh
from jax.sharding import PartitionSpec as P

D = 16384
HEAD = 128
GROUP = 16
KVW = 2
L = 256
KEEP = 16
TOKENS = 2048
SEQ = 4
FSDP = 32
GT = TOKENS // SEQ
FW = D // FSDP
ROWS = GT // FSDP
QW = KEEP * HEAD
KV = KVW * HEAD
STEP = 4

epsilon = 1e-05

AXES = ("yh", "core", "z", "x", "yl")
SIZES = (2, 2, 4, 4, 2)
TOK_AXES = ("yl", "z", "x")


bf16 = jnp.bfloat16
f32 = jnp.float32


def permute(array, move):
    places = np.array(list(np.ndindex(*SIZES)))
    pairs = [
        (int(np.ravel_multi_index(tuple(p), SIZES)), int(np.ravel_multi_index(move(*map(int, p)), SIZES)))
        for p in places
    ]
    return lax.ppermute(array, AXES, pairs)


def to_plane(yh, c, z, x, yl):
    return (z // 2, z % 2, (z + 2 * yh + c) % 4, x, yl)


def along_first(d):
    def move(yh, c, z, x, yl):
        return (yh, c, (z + d) % 4, x, yl) if c == 0 else (yh, c, z, (x + d) % 4, yl)

    return move


def along_second(d):
    def move(yh, c, z, x, yl):
        return (yh, c, z, (x + d) % 4, yl) if c == 0 else (yh, c, (z + d) % 4, x, yl)

    return move


def along_x(d):
    return lambda yh, c, z, x, yl: (yh, c, z, (x + d) % 4, yl)


def along_z(d):
    return lambda yh, c, z, x, yl: (yh, c, (z + d) % 4, x, yl)


def other_yl(yh, c, z, x, yl):
    return (yh, c, z, x, 1 - yl)


def other_yh(yh, c, z, x, yl):
    return (1 - yh, c, z, x, yl)


def other_core(yh, c, z, x, yl):
    return (yh, 1 - c, z, x, yl)


def narrow_kernel(h, g, wk, wv, ks, vs, out, hg):
    hf = h[...].astype(f32)
    hg[...] = (hf * g[...]).astype(bf16)
    square = jnp.sum(hf * hf, axis=1, keepdims=True)
    high = square.astype(bf16).astype(f32)
    lane = lax.broadcasted_iota(jnp.int32, (GT, 128), 1)
    pad = jnp.where(lane == 0, high, jnp.where(lane == 1, square - high, 0.0))
    out[:, 2 * KV :] = pad.astype(bf16)
    key = jnp.dot(hg[...], wk[...], preferred_element_type=f32) * ks[...]
    out[:, :KV] = key.astype(bf16)
    value = jnp.dot(hg[...], wv[...], preferred_element_type=f32) * vs[...]
    out[:, KV : 2 * KV] = value.astype(bf16)


def wide_kernel(kept, hg, *refs):
    ws, ss, (out,) = refs[:STEP], refs[STEP : 2 * STEP], refs[2 * STEP :]
    w = jnp.concatenate([r[...] for r in ws], axis=1)
    s = jnp.concatenate([r[0] for r in ss], axis=1)
    out[...] = (jnp.dot(hg[...], w, preferred_element_type=f32) * s).astype(bf16)


def wide(kept, hg, wq, qs):
    head = lambda i: pl.BlockSpec((FW, HEAD), lambda j, kept: (0, kept[STEP * j + i]))
    scale = lambda i: pl.BlockSpec((1, 1, HEAD), lambda j, kept: (kept[STEP * j + i], 0, 0))
    return pl.pallas_call(
        wide_kernel,
        out_shape=jax.ShapeDtypeStruct((GT, QW), bf16),
        grid_spec=pltpu.PrefetchScalarGridSpec(
            num_scalar_prefetch=1,
            grid=(KEEP // STEP,),
            in_specs=[pl.BlockSpec((GT, FW), lambda j, kept: (0, 0))]
            + [head(i) for i in range(STEP)]
            + [scale(i) for i in range(STEP)],
            out_specs=pl.BlockSpec((GT, STEP * HEAD), lambda j, kept: (0, j)),
        ),
    )(kept, hg, *[wq] * STEP, *[qs.reshape(-1, 1, HEAD)] * STEP)


def summed(x, j):
    return jnp.sum(x[:, :, j * 128 : (j + 1) * 128].astype(f32), axis=0)


def rotated(v, cosine, sine):
    return (v * cosine + pltpu.roll(v, 64, axis=1) * sine).astype(bf16)


def keys_kernel(x, cosine, sine, kv, inverse):
    last = summed(x, 2 * KVW)
    inv = lax.rsqrt((last[:, 0:1] + last[:, 1:2]) / D + epsilon)
    inverse[...] = jnp.broadcast_to(inv, (ROWS, 128))
    for j in range(2 * KVW):
        v = summed(x, j) * inv
        part = rotated(v, cosine[...], sine[...]) if j < KVW else v.astype(bf16)
        kv[:, j * 128 : (j + 1) * 128] = part


def attend_kernel(x, inverse, cosine, sine, kva, kvb, kvc, kvd, place, low, high, out):
    kv = jnp.concatenate([r[...].reshape(4 * ROWS, 2 * KV) for r in (kva, kvb, kvc, kvd)], axis=0)
    cos, sin = cosine[...] * inverse[...], sine[...] * inverse[...]
    qs = jnp.concatenate([rotated(summed(x, h), cos, sin) for h in range(KEEP)], axis=0)
    keys = jnp.concatenate([kv[:, g * HEAD : (g + 1) * HEAD] for g in range(KVW)], axis=0)
    values = jnp.concatenate([kv[:, KV + g * HEAD : KV + (g + 1) * HEAD] for g in range(KVW)], axis=0)
    scores = lax.dot_general(qs, keys, (((1,), (1,)), ((), ())), preferred_element_type=f32)
    scores = scores * np.float32(1.0 / np.sqrt(HEAD))
    seen = (place[...] >= low[...]) & (place[...] <= high[...])
    scores = jnp.where(seen, scores, -1e30)
    top = jnp.max(scores, axis=1, keepdims=True)
    e = jnp.where(seen, jnp.exp(scores - top), 0.0)
    weights = (e / jnp.sum(e, axis=1, keepdims=True)).astype(bf16)
    att = jnp.dot(weights, values, preferred_element_type=f32).astype(bf16)
    for h in range(KEEP):
        part = att[h * ROWS : (h + 1) * ROWS]
        out[:, :, h * HEAD : (h + 1) * HEAD] = jnp.broadcast_to(part[None], (FSDP, ROWS, HEAD))


def mix_kernel(kept, att, *refs):
    ws, refs = refs[:STEP], refs[STEP:]
    scale, h, gain, residual, gained, acc = refs
    j = pl.program_id(0)
    a = att[:, pl.ds(pl.multiple_of(j * STEP * HEAD, STEP * HEAD), STEP * HEAD)]
    w = jnp.concatenate([r[...] for r in ws], axis=0)
    part = jnp.dot(a, w, preferred_element_type=f32)

    @pl.when(j == 0)
    def _():
        acc[...] = part

    @pl.when(j > 0)
    def _():
        acc[...] += part

    @pl.when(j == KEEP // STEP - 1)
    def _():
        r = (h[...].astype(f32) + acc[...] * scale[...]).astype(bf16)
        residual[...] = r
        gained[...] = (r.astype(f32) * gain[...]).astype(bf16)


def mix(kept, att, w_out, out_scale, h, gain):
    whole = lambda shape: pl.BlockSpec(shape, lambda j, kept: (0,) * len(shape))
    head = lambda i: pl.BlockSpec((HEAD, FW), lambda j, kept: (kept[STEP * j + i], 0))
    return pl.pallas_call(
        mix_kernel,
        out_shape=[jax.ShapeDtypeStruct((GT, FW), bf16)] * 2,
        grid_spec=pltpu.PrefetchScalarGridSpec(
            num_scalar_prefetch=1,
            grid=(KEEP // STEP,),
            in_specs=[
                whole((GT, QW)),
                *[head(i) for i in range(STEP)],
                whole((1, FW)),
                whole((GT, FW)),
                whole((1, FW)),
            ],
            out_specs=[whole((GT, FW))] * 2,
            scratch_shapes=[pltpu.VMEM((GT, FW), f32)],
        ),
    )(kept, att, *[w_out] * STEP, out_scale[None], h, gain[None])


def moment_kernel(count, stage, *refs):
    table, refs = refs[0], refs[1:]
    lhs, refs = (refs[:4], refs[4:]) if stage == 0 else ((), refs)
    groups, refs = refs[:count], refs[count:]
    if stage == 0:
        left, out, held, held_sem, out_sem, acc = refs
    elif stage == 1:
        left, acc, held, held_sem, out_sem = refs
    else:
        left, _, _, acc, out, held, held_sem, out_sem = refs

    chunks = [pltpu.make_async_copy(groups[i], held.at[i], held_sem.at[i]) for i in range(count)]
    reads = [pltpu.make_async_copy(lhs[i], left.at[i], out_sem.at[i]) for i in range(len(lhs))]
    for copy in reads + chunks[:3]:
        copy.start()
    if stage < 2:
        acc[...] = jnp.zeros_like(acc)
    for copy in reads:
        copy.wait()
    for i in range(count):
        chunks[i].wait()
        if i + 3 < count:
            chunks[i + 3].start()
        for k in range(2):
            group, block = table[2 * i + k, 0], table[2 * i + k, 1]
            acc[block] += jnp.dot(left[group], held[i, k], preferred_element_type=f32)
    if stage == 1:
        return
    writes = []
    for n in range(4):
        block = 2 * n + table[2 * count, 0]
        strip = out.at[:, pl.ds(pl.multiple_of(block * FW, FW), FW)]
        writes.append(pltpu.make_async_copy(acc.at[n], strip, out_sem.at[n]))
        writes[-1].start()
    for copy in writes:
        copy.wait()


def moment(table, groups, state, stage):
    count = len(groups)
    anywhere = pl.BlockSpec(memory_space=pl.ANY)
    vmem = pl.BlockSpec(memory_space=pltpu.VMEM)
    left = pltpu.VMEM((4, FW, GT), bf16)
    sums = pltpu.VMEM((4, FW, FW), f32)
    hessian = jax.ShapeDtypeStruct((FW, D // SEQ), f32)
    scratch = [
        pltpu.VMEM((count, 2, GT, FW), bf16),
        pltpu.SemaphoreType.DMA((count,)),
        pltpu.SemaphoreType.DMA((4,)),
    ]
    if stage == 0:
        operands, specs = [*state, *groups], [anywhere] * (4 + count)
        out_shape, out_specs, aliases = [left, hessian], [vmem, anywhere], {}
        scratch.append(sums)
    elif stage == 1:
        operands, specs = [*groups, near(state[0])], [anywhere] * count + [vmem]
        out_shape, out_specs, aliases = [sums], [vmem], {}
    else:
        operands = [*groups, near(state[0]), near(state[1]), state[2]]
        specs = [anywhere] * count + [vmem, vmem, anywhere]
        out_shape, out_specs, aliases = [sums, hessian], [vmem, anywhere], {count + 2: 0, count + 3: 1}
    return pl.pallas_call(
        lambda *refs: moment_kernel(count, stage, *refs),
        out_shape=out_shape,
        in_specs=[pl.BlockSpec(memory_space=pltpu.SMEM)] + specs,
        out_specs=out_specs,
        scratch_shapes=scratch,
        input_output_aliases=aliases,
        compiler_params=pltpu.CompilerParams(vmem_limit_bytes=24 << 20),
    )(table, *operands)


def near(array):
    return pltpu.with_memory_space_constraint(array, pltpu.VMEM)


def shards(
    hidden_in,
    gain_in,
    w_query,
    query_scale,
    w_key,
    key_scale,
    w_value,
    value_scale,
    w_out,
    out_scale,
    gain_mid,
    head_order,
):
    yh, core, z, x, yl = (lax.axis_index(a) for a in AXES)
    kept = head_order[:KEEP]

    narrow, hg = pl.pallas_call(
        narrow_kernel,
        out_shape=[jax.ShapeDtypeStruct((GT, 2 * KV + 128), bf16), jax.ShapeDtypeStruct((GT, FW), bf16)],
    )(hidden_in, gain_in[None], w_key, w_value, key_scale[None], value_scale[None])
    narrow = lax.all_to_all(narrow.reshape(FSDP, ROWS, 2 * KV + 128), TOK_AXES, split_axis=0, concat_axis=0, tiled=True)
    query = wide(kept, hg, w_query, query_scale).reshape(FSDP, ROWS, QW)
    query = lax.all_to_all(query, TOK_AXES, split_axis=0, concat_axis=0, tiled=True)

    positions = (z * 4 + x) * ROWS + jnp.arange(ROWS, dtype=jnp.int32)
    steps = jnp.arange(HEAD // 2, dtype=f32)
    frequency = jnp.exp(-jnp.log(jnp.float32(500000.0)) * steps * 2.0 / HEAD)
    angles = positions.astype(f32)[:, None] * frequency[None, :]
    cosine = jnp.cos(angles)
    sine = jnp.sin(angles)
    cosine = jnp.concatenate([cosine, cosine], axis=1)
    sine = jnp.concatenate([-sine, sine], axis=1)
    kv_own, inverse = pl.pallas_call(
        keys_kernel,
        out_shape=[jax.ShapeDtypeStruct((ROWS, 2 * KV), bf16), jax.ShapeDtypeStruct((ROWS, 128), f32)],
    )(near(narrow), cosine, sine)
    kv = jnp.stack([kv_own] + [permute(kv_own, along_x(d)) for d in (1, -1, 2)])
    kv = [kv] + [permute(kv, along_z(d)) for d in (1, -1, 2)]

    offsets = np.array([0, -1, 1, 2], np.int32)
    block = ((z + offsets) % 4)[:, None] * 4 + ((x + offsets) % 4)[None, :]
    place = block.reshape(-1, 1) * ROWS + np.arange(ROWS, dtype=np.int32)[None, :]
    place = place.reshape(1, L) + np.arange(KVW, dtype=np.int32)[:, None] * L
    low = jnp.repeat(kept // GROUP * L, ROWS)[:, None]
    high = low + jnp.tile(positions, KEEP)[:, None]
    attended = pl.pallas_call(
        attend_kernel,
        out_shape=jax.ShapeDtypeStruct((FSDP, ROWS, QW), bf16),
    )(near(query), inverse, cosine, sine, *kv, place.reshape(1, KVW * L), low, high)
    attended = lax.all_to_all(attended, TOK_AXES, split_axis=0, concat_axis=0, tiled=True)
    residual, gained = mix(kept, attended.reshape(GT, QW), w_out, out_scale, hidden_in, gain_mid)

    resid_f = residual.astype(f32)
    square = jnp.sum(resid_f * resid_f, axis=1)
    square = jnp.broadcast_to(square[None, None], (FSDP, 1, GT))
    square = lax.all_to_all(square, TOK_AXES, split_axis=0, concat_axis=0, tiled=True)

    own = permute(gained, to_plane)
    other = permute(own, other_yl)
    a = [own] + [permute(own, along_first(d)) for d in (1, -1, 2)]
    pieces = {(0, 0, half): jnp.stack(a[2 * half : 2 * half + 2]) for half in range(2)}
    pieces[1, 0, 0] = jnp.stack([other, permute(a[1], other_yl)])
    pieces[1, 0, 1] = permute(pieces[0, 0, 1], other_yl)
    for e in range(2):
        for half in range(2):
            for b, d in ((1, 1), (2, -1)):
                pieces[e, b, half] = permute(pieces[e, 0, half], along_second(d))
        pieces[e, 3, 0] = permute(pieces[e, 1, 0], along_second(1))
        far = (pieces[0, 2, 1], along_second(-1)) if e == 0 else (pieces[0, 3, 1], other_yl)
        pieces[e, 3, 1] = permute(*far)

    square = square.sum(axis=(0, 1))
    weight = 1.0 / ((square / D + epsilon) * TOKENS)
    rows = (gained.T.astype(f32) * weight[None, :]).astype(bf16)
    rows_yh = permute(rows, other_yh)
    lhs = [rows, rows_yh, permute(rows, other_core), permute(rows_yh, other_core)]

    first_at = jnp.where(core == 0, z, x)
    second_at = jnp.where(core == 0, x, z)

    def table_of(keys):
        e, b, i = (np.array([k[j] if j < 2 else 2 * k[2] + n for k in keys for n in range(2)]) for j in range(3))
        first = (first_at + offsets[i]) % 4
        second = (second_at + offsets[b]) % 4
        group = (jnp.where(core == 0, first, second) - 2 * yh - core) % 4
        x_at = jnp.where(core == 0, second, first)
        left = (group // 2 != yh).astype(jnp.int32) + 2 * (group % 2 != core).astype(jnp.int32)
        half = yl if e[0] == 0 else 1 - yl
        return jnp.concatenate([jnp.stack([left, x_at], axis=1), jnp.full((1, 2), half)]).astype(jnp.int32)

    keys = [
        [(0, b, half) for b in range(4) for half in range(2)],
        [(1, 0, 0), (1, 0, 1), (1, 1, 0), (1, 2, 0), (1, 2, 1), (1, 3, 1)],
        [(1, 1, 1), (1, 3, 0)],
    ]
    tables = [table_of(k) for k in keys]
    groups = [[pieces[k] for k in ks] for ks in keys]
    left, hessian = moment(tables[0], groups[0], lhs, 0)
    (sums,) = moment(tables[1], groups[1], [left], 1)
    _, hessian = moment(tables[2], groups[2], [left, sums, hessian], 2)
    return (hessian, residual)


def solution(mesh):
    fine = Mesh(mesh.devices.reshape(SIZES), AXES)
    seq = ("yh", "core")
    fsdp = ("z", "x", "yl")
    return jax.shard_map(
        shards,
        mesh=fine,
        in_specs=(
            P(seq, fsdp),
            P(fsdp),
            P(fsdp, None),
            P(),
            P(fsdp, None),
            P(),
            P(fsdp, None),
            P(),
            P(None, fsdp),
            P(fsdp),
            P(fsdp),
            P(),
        ),
        out_specs=(P(fsdp, seq), P(seq, fsdp)),
        check_vma=False,
    )
```

profile of v0, /device:TPU:24, one launch (start us, length us, event | category | flops | bytes accessed | tf_op | source)
XLA Modules:
  0.0 240.9 jit_solution(4071541431830441525)
XLA Ops:
  3.1 9.4 %all-to-all-start.1 = ((bf16[32,16,640]{2,1,0:T(8,128)(2,1)}), bf16[32,16,640]{2,1,0:T(8,128)(2,1)S(1)}, u32[]{:S(2)}, u32[]{:S(2)}) async-start(bf16[32,16,640]{2,1,0:T(8,128)(2,1)} %bitcast.39), calls=%async_computation.1 | async-start | bytes 1310720 | tf_op jit(solution)/shard_map/all_to_all | solution.py:301
  13.8 5.8 %shard_map.213 = bf16[512,2048]{1,0:T(8,128)(2,1)} custom-call(s32[16]{0:T(128)} %get-tuple-element.33.kept, bf16[512,512]{1,0:T(8,128)(2,1)} %get-tuple-element.11.hg, bf16[512,4096]{1,0:T(8,128)(2,1)} %refs_3_.2, bf16[512,4096]{1,0:T(8,128)(2,1)} %refs_3_.2, bf16[512,4096]{1,0:T(8,128)(2,1)} %refs_3_.2, bf16[512,4096]{1,0:T(8,128)(2,1)} %refs_3_.2, ...), custom_call_target="tpu_custom_call" | custom-call | tf_op jit(solution)/shard_map/pallas_call | solution.py:108
  19.6 5.1 %all-to-all-done.1.x = bf16[32,16,640]{2,1,0:T(8,128)(2,1)S(1)} async-done(((bf16[32,16,640]{2,1,0:T(8,128)(2,1)}), bf16[32,16,640]{2,1,0:T(8,128)(2,1)S(1)}, u32[]{:S(2)}, u32[]{:S(2)}) %all-to-all-start.1) | async-done | bytes 655392 | tf_op jit(solution)/shard_map/all_to_all | solution.py:301
  24.7 4.9 %all-to-all-start = ((bf16[32,16,2048]{2,1,0:T(8,128)(2,1)}), bf16[32,16,2048]{2,1,0:T(8,128)(2,1)S(1)}, u32[]{:S(2)}, u32[]{:S(2)}) async-start(bf16[32,16,2048]{2,1,0:T(8,128)(2,1)} %bitcast.38), calls=%async_computation | async-start | bytes 4194304 | tf_op jit(solution)/shard_map/all_to_all | solution.py:303
  33.0 3.0 %collective-permute-start.2 = (bf16[16,512]{1,0:T(8,128)(2,1)}, bf16[16,512]{1,0:T(8,128)(2,1)S(1)}, u32[]{:S(2)}, u32[]{:S(2)}) collective-permute-start(bf16[16,512]{1,0:T(8,128)(2,1)} %get-tuple-element.14), channel_id=1, source_target_pairs={{0,4},{1,5},{2,6},{3,7},{4,0},{5,1},{6,2},{7,3},{8,12},{9,13},{10,... | collective-permute-start | bytes 49160 | tf_op jit(solution)/shard_map/ppermute | solution.py:43
  38.0 16.9 %collective-permute-done.2 = bf16[16,512]{1,0:T(8,128)(2,1)S(1)} collective-permute-done((bf16[16,512]{1,0:T(8,128)(2,1)}, bf16[16,512]{1,0:T(8,128)(2,1)S(1)}, u32[]{:S(2)}, u32[]{:S(2)}) %collective-permute-start.2) | collective-permute-done | bytes 16416 | tf_op jit(solution)/shard_map/ppermute | solution.py:43
  55.7 3.6 %collective-permute-start.5 = (bf16[4,16,512]{2,1,0:T(8,128)(2,1)S(1)}, bf16[4,16,512]{2,1,0:T(8,128)(2,1)S(1)}, u32[]{:S(2)}, u32[]{:S(2)}) collective-permute-start(bf16[4,16,512]{2,1,0:T(8,128)(2,1)S(1)} %pad_maximum_fusion.3.kva), channel_id=1, source_target_pairs={{0,16},{1,17},{2,18},{3,19},{4,20},{5,21},{6,22},{7,23},{8,24},{9,... | collective-permute-start | bytes 196616 | tf_op jit(solution)/shard_map/ppermute | solution.py:43
  66.5 3.8 %shard_map.215 = bf16[32,16,2048]{2,1,0:T(8,128)(2,1)} custom-call(bf16[32,16,2048]{2,1,0:T(8,128)(2,1)S(1)} %all-to-all-done.x, f32[16,128]{1,0:T(8,128)} %get-tuple-element.13.inverse, f32[16,128]{1,0:T(8,128)} %pad_maximum_fusion.4.cosine, f32[16,128]{1,0:T(8,128)} %pad_maximum_fusion.5.sine, bf16[4,16,512]{2,1,0:T(8,128)(2,1)} %copy-done.10, ...), custom_call_target="tpu_custom_call" | custom-call | tf_op jit(solution)/shard_map/pallas_call | solution.py:326
  70.3 29.5 %all_to_all.20 = bf16[32,16,2048]{2,1,0:T(8,128)(2,1)} all-to-all(bf16[32,16,2048]{2,1,0:T(8,128)(2,1)} %shard_map.215), channel_id=1, replica_groups=mesh['yh'=2,'core'=2,'z'=4,'x'=4,'yl'=2] {'yl','z','x'}, dimensions={0} | all-to-all | bytes 4194304 | tf_op jit(solution)/shard_map/all_to_all | solution.py:330
  99.8 6.6 %shard_map.216 = (bf16[512,512]{1,0:T(8,128)(2,1)}, bf16[512,512]{1,0:T(8,128)(2,1)}) custom-call(s32[16]{0:T(128)} %get-tuple-element.33.kept, bf16[512,2048]{1,0:T(8,128)(2,1)} %bitcast.37, bf16[4096,512]{1,0:T(8,128)(2,1)} %refs_3_.3, bf16[4096,512]{1,0:T(8,128)(2,1)} %refs_3_.3, bf16[4096,512]{1,0:T(8,128)(2,1)} %refs_3_.3, bf16[4096,512]{1,0:T(8,128)(2,1)} %refs_3_.3, ...), custom_call_target="tpu_custom_call" | custom-call | tf_op jit(solution)/shard_map/pallas_call | solution.py:185
  106.4 3.7 %collective-permute-start.6 = (bf16[512,512]{1,0:T(8,128)(2,1)}, bf16[512,512]{1,0:T(8,128)(2,1)S(1)}, u32[]{:S(2)}, u32[]{:S(2)}) collective-permute-start(bf16[512,512]{1,0:T(8,128)(2,1)} %get-tuple-element.15), channel_id=1, source_target_pairs={{0,0},{1,1},{2,2},{3,3},{4,4},{5,5},{6,6},{7,7},{8,40},{9,41},{10,... | collective-permute-start | bytes 1572872 | tf_op jit(solution)/shard_map/ppermute | solution.py:43
  112.0 5.5 %all-to-all-start.3 = ((f32[32,1,512]{2,1,0:T(1,128)}), f32[32,1,512]{2,1,0:T(1,128)S(1)}, u32[]{:S(2)}, u32[]{:S(2)}) async-start(f32[32,1,512]{2,1,0:T(1,128)} %broadcast_in_dim.38), calls=%async_computation.3 | async-start | bytes 131072 | tf_op jit(solution)/shard_map/all_to_all | solution.py:336
  118.8 6.2 %all-to-all-done.3 = f32[32,1,512]{2,1,0:T(1,128)S(1)} async-done(((f32[32,1,512]{2,1,0:T(1,128)}), f32[32,1,512]{2,1,0:T(1,128)S(1)}, u32[]{:S(2)}, u32[]{:S(2)}) %all-to-all-start.3) | async-done | bytes 65568 | tf_op jit(solution)/shard_map/all_to_all | solution.py:336
  133.1 8.1 %collective-permute-done.12 = bf16[512,512]{1,0:T(8,128)(2,1)S(1)} collective-permute-done((bf16[512,512]{1,0:T(8,128)(2,1)S(1)}, bf16[512,512]{1,0:T(8,128)(2,1)S(1)}, u32[]{:S(2)}, u32[]{:S(2)}) %collective-permute-start.12) | collective-permute-done | bytes 524320 | tf_op jit(solution)/shard_map/ppermute | solution.py:43
  146.0 5.3 %collective-permute-start.22 = (bf16[2,512,512]{2,1,0:T(8,128)(2,1)S(1)}, bf16[2,512,512]{2,1,0:T(8,128)(2,1)}, u32[]{:S(2)}, u32[]{:S(2)}) collective-permute-start(bf16[2,512,512]{2,1,0:T(8,128)(2,1)S(1)} %pad_maximum_fusion.refs_6_), channel_id=1, source_target_pairs={{0,6},{1,7},{2,0},{3,1},{4,2},{5,3},{6,4},{7,5},{8,14},{9,15},{10,... | collective-permute-start | bytes 3145736 | tf_op jit(solution)/shard_map/ppermute | solution.py:43
  151.4 5.7 %collective-permute-done.11 = bf16[512,512]{1,0:T(8,128)(2,1)S(1)} collective-permute-done((bf16[512,512]{1,0:T(8,128)(2,1)S(1)}, bf16[512,512]{1,0:T(8,128)(2,1)S(1)}, u32[]{:S(2)}, u32[]{:S(2)}) %collective-permute-start.11) | collective-permute-done | bytes 524320 | tf_op jit(solution)/shard_map/ppermute | solution.py:43
  157.1 7.6 %collective-permute-done.13 = bf16[512,512]{1,0:T(8,128)(2,1)S(1)} collective-permute-done((bf16[512,512]{1,0:T(8,128)(2,1)S(1)}, bf16[512,512]{1,0:T(8,128)(2,1)S(1)}, u32[]{:S(2)}, u32[]{:S(2)}) %collective-permute-start.13) | collective-permute-done | bytes 524320 | tf_op jit(solution)/shard_map/ppermute | solution.py:43
  175.4 6.3 %collective-permute-done.20.refs_8_ = bf16[2,512,512]{2,1,0:T(8,128)(2,1)} collective-permute-done((bf16[2,512,512]{2,1,0:T(8,128)(2,1)S(1)}, bf16[2,512,512]{2,1,0:T(8,128)(2,1)}, u32[]{:S(2)}, u32[]{:S(2)}) %collective-permute-start.20) | collective-permute-done | bytes 1048608 | tf_op jit(solution)/shard_map/ppermute | solution.py:43
  181.7 11.6 %collective-permute-done.9.refs_2_ = bf16[2,512,512]{2,1,0:T(8,128)(2,1)} collective-permute-done((bf16[2,512,512]{2,1,0:T(8,128)(2,1)S(1)}, bf16[2,512,512]{2,1,0:T(8,128)(2,1)}, u32[]{:S(2)}, u32[]{:S(2)}) %collective-permute-start.9) | collective-permute-done | bytes 1048608 | tf_op jit(solution)/shard_map/ppermute | solution.py:43
  195.3 8.9 %collective-permute-done.23.refs_11_ = bf16[2,512,512]{2,1,0:T(8,128)(2,1)} collective-permute-done((bf16[2,512,512]{2,1,0:T(8,128)(2,1)}, bf16[2,512,512]{2,1,0:T(8,128)(2,1)}, u32[]{:S(2)}, u32[]{:S(2)}) %collective-permute-start.23) | collective-permute-done | bytes 1048608 | tf_op jit(solution)/shard_map/ppermute | solution.py:43
  212.5 9.2 %shard_map.217 = (bf16[4,512,512]{2,1,0:T(8,128)(2,1)S(1)}, f32[512,4096]{1,0:T(8,128)}) custom-call(s32[17,2]{1,0:T(8,128)S(1)} %concatenate.18.refs_0_, bf16[512,512]{1,0:T(8,128)(2,1)S(1)} %copy-done.1, bf16[512,512]{1,0:T(8,128)(2,1)S(1)} %copy-done.5, bf16[512,512]{1,0:T(8,128)(2,1)S(1)} %copy-done.7, bf16[512,512]{1,0:T(8,128)(2,1)S(1)} %copy-done.9, ...), custom_call_target="tpu_custom_call" | custom-call | tf_op jit(solution)/shard_map/pallas_call | solution.py:265
  221.7 8.1 %collective-permute-done.27.refs_6_ = bf16[2,512,512]{2,1,0:T(8,128)(2,1)} collective-permute-done((bf16[2,512,512]{2,1,0:T(8,128)(2,1)}, bf16[2,512,512]{2,1,0:T(8,128)(2,1)}, u32[]{:S(2)}, u32[]{:S(2)}) %collective-permute-start.27) | collective-permute-done | bytes 1048608 | tf_op jit(solution)/shard_map/ppermute | solution.py:43
  229.8 5.6 %shard_map.218.refs_4_ = f32[4,512,512]{2,1,0:T(8,128)S(1)} custom-call(s32[13,2]{1,0:T(8,128)S(1)} %concatenate.19.refs_0_, bf16[2,512,512]{2,1,0:T(8,128)(2,1)S(1)} %pad_maximum_fusion.1.refs_1_, bf16[2,512,512]{2,1,0:T(8,128)(2,1)} %collective-permute-done.9.refs_2_, bf16[2,512,512]{2,1,0:T(8,128)(2,1)} %collective-permute-done.14.refs_3_, ...), custom_call_target="tpu_custom_call" | custom-call | tf_op jit(solution)/shard_map/pallas_call | solution.py:265
  235.4 5.3 %shard_map.219 = (f32[4,512,512]{2,1,0:T(8,128)S(1)}, f32[512,4096]{1,0:T(8,128)}) custom-call(s32[5,2]{1,0:T(8,128)S(1)} %concatenate.15.refs_0_, bf16[2,512,512]{2,1,0:T(8,128)(2,1)} %collective-permute-done.10.refs_1_, bf16[2,512,512]{2,1,0:T(8,128)(2,1)} %collective-permute-done.15.refs_2_, ...), custom_call_target="tpu_custom_call", output_to_operand_aliasing={{0}: (4, {}), {1}: (5, {})} | custom-call | tf_op jit(solution)/shard_map/pallas_call | solution.py:265
  (136 shorter events, 54.2 us)
Async XLA Ops:
  3.1 21.6 %all-to-all-start.1 = ((bf16[32,16,640]{2,1,0:T(8,128)(2,1)}), bf16[32,16,640]{2,1,0:T(8,128)(2,1)S(1)}, u32[]{:S(2)}, u32[]{:S(2)}) async-start(bf16[32,16,640]{2,1,0:T(8,128)(2,1)} %bitcast.39), calls=%async_computation.1 | async-start | bytes 1310720 | tf_op jit(solution)/shard_map/all_to_all | solution.py:301
  24.7 41.2 %all-to-all-start = ((bf16[32,16,2048]{2,1,0:T(8,128)(2,1)}), bf16[32,16,2048]{2,1,0:T(8,128)(2,1)S(1)}, u32[]{:S(2)}, u32[]{:S(2)}) async-start(bf16[32,16,2048]{2,1,0:T(8,128)(2,1)} %bitcast.38), calls=%async_computation | async-start | bytes 4194304 | tf_op jit(solution)/shard_map/all_to_all | solution.py:303
  33.0 21.9 %collective-permute-start.2 = (bf16[16,512]{1,0:T(8,128)(2,1)}, bf16[16,512]{1,0:T(8,128)(2,1)S(1)}, u32[]{:S(2)}, u32[]{:S(2)}) collective-permute-start(bf16[16,512]{1,0:T(8,128)(2,1)} %get-tuple-element.14), channel_id=1, source_target_pairs={{0,4},{1,5},{2,6},{3,7},{4,0},{5,1},{6,2},{7,3},{8,12},{9,13},{10,... | collective-permute-start | bytes 49160 | tf_op jit(solution)/shard_map/ppermute | solution.py:43
  35.9 19.0 %collective-permute-start.1 = (bf16[16,512]{1,0:T(8,128)(2,1)}, bf16[16,512]{1,0:T(8,128)(2,1)S(1)}, u32[]{:S(2)}, u32[]{:S(2)}) collective-permute-start(bf16[16,512]{1,0:T(8,128)(2,1)} %get-tuple-element.14), channel_id=1, source_target_pairs={{0,6},{1,7},{2,0},{3,1},{4,2},{5,3},{6,4},{7,5},{8,14},{9,15},{10,... | collective-permute-start | bytes 49160 | tf_op jit(solution)/shard_map/ppermute | solution.py:43
  37.1 17.8 %collective-permute-start = (bf16[16,512]{1,0:T(8,128)(2,1)}, bf16[16,512]{1,0:T(8,128)(2,1)S(1)}, u32[]{:S(2)}, u32[]{:S(2)}) collective-permute-start(bf16[16,512]{1,0:T(8,128)(2,1)} %get-tuple-element.14), channel_id=1, source_target_pairs={{0,2},{1,3},{2,4},{3,5},{4,6},{5,7},{6,0},{7,1},{8,10},{9,11},{10,... | collective-permute-start | bytes 49160 | tf_op jit(solution)/shard_map/ppermute | solution.py:43
  106.4 18.7 %collective-permute-start.6 = (bf16[512,512]{1,0:T(8,128)(2,1)}, bf16[512,512]{1,0:T(8,128)(2,1)S(1)}, u32[]{:S(2)}, u32[]{:S(2)}) collective-permute-start(bf16[512,512]{1,0:T(8,128)(2,1)} %get-tuple-element.15), channel_id=1, source_target_pairs={{0,0},{1,1},{2,2},{3,3},{4,4},{5,5},{6,6},{7,7},{8,40},{9,41},{10,... | collective-permute-start | bytes 1572872 | tf_op jit(solution)/shard_map/ppermute | solution.py:43
  125.1 16.1 %collective-permute-start.12 = (bf16[512,512]{1,0:T(8,128)(2,1)S(1)}, bf16[512,512]{1,0:T(8,128)(2,1)S(1)}, u32[]{:S(2)}, u32[]{:S(2)}) collective-permute-start(bf16[512,512]{1,0:T(8,128)(2,1)S(1)} %collective-permute-done.6), channel_id=1, source_target_pairs={{0,8},{1,9},{2,10},{3,11},{4,12},{5,13},{6,14},{7,15},{8,16},{9,17... | collective-permute-start | bytes 1572872 | tf_op jit(solution)/shard_map/ppermute | solution.py:43
  125.5 17.5 %collective-permute-start.8 = (bf16[512,512]{1,0:T(8,128)(2,1)S(1)}, bf16[512,512]{1,0:T(8,128)(2,1)S(1)}, u32[]{:S(2)}, u32[]{:S(2)}) collective-permute-start(bf16[512,512]{1,0:T(8,128)(2,1)S(1)} %collective-permute-done.6), channel_id=1, source_target_pairs={{0,16},{1,17},{2,18},{3,19},{4,20},{5,21},{6,22},{7,23},{8,24},{9,... | collective-permute-start | bytes 1572872 | tf_op jit(solution)/shard_map/ppermute | solution.py:43
  129.7 16.4 %collective-permute-start.16 = (bf16[512,512]{1,0:T(8,128)(2,1)S(1)}, bf16[512,512]{1,0:T(8,128)(2,1)S(1)}, u32[]{:S(2)}, u32[]{:S(2)}) collective-permute-start(bf16[512,512]{1,0:T(8,128)(2,1)S(1)} %fusion.refs_1_), channel_id=1, source_target_pairs={{0,64},{1,65},{2,66},{3,67},{4,68},{5,69},{6,70},{7,71},{8,72},{9,... | collective-permute-start | bytes 1572872 | tf_op jit(solution)/shard_map/ppermute | solution.py:43
  132.6 24.5 %collective-permute-start.11 = (bf16[512,512]{1,0:T(8,128)(2,1)S(1)}, bf16[512,512]{1,0:T(8,128)(2,1)S(1)}, u32[]{:S(2)}, u32[]{:S(2)}) collective-permute-start(bf16[512,512]{1,0:T(8,128)(2,1)S(1)} %collective-permute-done.6), channel_id=1, source_target_pairs={{0,1},{1,0},{2,3},{3,2},{4,5},{5,4},{6,7},{7,6},{8,9},{9,8},{10,11... | collective-permute-start | bytes 1572872 | tf_op jit(solution)/shard_map/ppermute | solution.py:43
  141.2 28.5 %collective-permute-start.21 = (bf16[2,512,512]{2,1,0:T(8,128)(2,1)S(1)}, bf16[2,512,512]{2,1,0:T(8,128)(2,1)S(1)}, u32[]{:S(2)}, u32[]{:S(2)}) collective-permute-start(bf16[2,512,512]{2,1,0:T(8,128)(2,1)S(1)} %pad_maximum_fusion.2.refs_5_), channel_id=1, source_target_pairs={{0,6},{1,7},{2,0},{3,1},{4,2},{5,3},{6,4},{7,5},{8,14},{9,15},{10,... | collective-permute-start | bytes 3145736 | tf_op jit(solution)/shard_map/ppermute | solution.py:43
  142.9 29.0 %collective-permute-start.19 = (bf16[2,512,512]{2,1,0:T(8,128)(2,1)S(1)}, bf16[2,512,512]{2,1,0:T(8,128)(2,1)}, u32[]{:S(2)}, u32[]{:S(2)}) collective-permute-start(bf16[2,512,512]{2,1,0:T(8,128)(2,1)S(1)} %pad_maximum_fusion.2.refs_5_), channel_id=1, source_target_pairs={{0,2},{1,3},{2,4},{3,5},{4,6},{5,7},{6,0},{7,1},{8,10},{9,11},{10,... | collective-permute-start | bytes 3145736 | tf_op jit(solution)/shard_map/ppermute | solution.py:43
  143.3 21.3 %collective-permute-start.13 = (bf16[512,512]{1,0:T(8,128)(2,1)S(1)}, bf16[512,512]{1,0:T(8,128)(2,1)S(1)}, u32[]{:S(2)}, u32[]{:S(2)}) collective-permute-start(bf16[512,512]{1,0:T(8,128)(2,1)S(1)} %collective-permute-done.12), channel_id=1, source_target_pairs={{0,1},{1,0},{2,3},{3,2},{4,5},{5,4},{6,7},{7,6},{8,9},{9,8},{10,11... | collective-permute-start | bytes 1572872 | tf_op jit(solution)/shard_map/ppermute | solution.py:43
  146.0 26.9 %collective-permute-start.22 = (bf16[2,512,512]{2,1,0:T(8,128)(2,1)S(1)}, bf16[2,512,512]{2,1,0:T(8,128)(2,1)}, u32[]{:S(2)}, u32[]{:S(2)}) collective-permute-start(bf16[2,512,512]{2,1,0:T(8,128)(2,1)S(1)} %pad_maximum_fusion.refs_6_), channel_id=1, source_target_pairs={{0,6},{1,7},{2,0},{3,1},{4,2},{5,3},{6,4},{7,5},{8,14},{9,15},{10,... | collective-permute-start | bytes 3145736 | tf_op jit(solution)/shard_map/ppermute | solution.py:43
  165.6 16.1 %collective-permute-start.20 = (bf16[2,512,512]{2,1,0:T(8,128)(2,1)S(1)}, bf16[2,512,512]{2,1,0:T(8,128)(2,1)}, u32[]{:S(2)}, u32[]{:S(2)}) collective-permute-start(bf16[2,512,512]{2,1,0:T(8,128)(2,1)S(1)} %pad_maximum_fusion.refs_6_), channel_id=1, source_target_pairs={{0,2},{1,3},{2,4},{3,5},{4,6},{5,7},{6,0},{7,1},{8,10},{9,11},{10,... | collective-permute-start | bytes 3145736 | tf_op jit(solution)/shard_map/ppermute | solution.py:43
  167.4 25.9 %collective-permute-start.9 = (bf16[2,512,512]{2,1,0:T(8,128)(2,1)S(1)}, bf16[2,512,512]{2,1,0:T(8,128)(2,1)}, u32[]{:S(2)}, u32[]{:S(2)}) collective-permute-start(bf16[2,512,512]{2,1,0:T(8,128)(2,1)S(1)} %pad_maximum_fusion.refs_6_), channel_id=1, source_target_pairs={{0,1},{1,0},{2,3},{3,2},{4,5},{5,4},{6,7},{7,6},{8,9},{9,8},{10,11... | collective-permute-start | bytes 3145736 | tf_op jit(solution)/shard_map/ppermute | solution.py:43
  170.7 23.2 %collective-permute-start.14 = (bf16[2,512,512]{2,1,0:T(8,128)(2,1)S(1)}, bf16[2,512,512]{2,1,0:T(8,128)(2,1)}, u32[]{:S(2)}, u32[]{:S(2)}) collective-permute-start(bf16[2,512,512]{2,1,0:T(8,128)(2,1)S(1)} %pad_maximum_fusion.1.refs_1_), channel_id=1, source_target_pairs={{0,2},{1,3},{2,4},{3,5},{4,6},{5,7},{6,0},{7,1},{8,10},{9,11},{10,... | collective-permute-start | bytes 3145736 | tf_op jit(solution)/shard_map/ppermute | solution.py:43
  171.9 32.2 %collective-permute-start.23 = (bf16[2,512,512]{2,1,0:T(8,128)(2,1)}, bf16[2,512,512]{2,1,0:T(8,128)(2,1)}, u32[]{:S(2)}, u32[]{:S(2)}) collective-permute-start(bf16[2,512,512]{2,1,0:T(8,128)(2,1)} %collective-permute-done.19.refs_7_), channel_id=1, source_target_pairs={{0,2},{1,3},{2,4},{3,5},{4,6},{5,7},{6,0},{7,1},{8,10},{9,11},{10,... | collective-permute-start | bytes 3145736 | tf_op jit(solution)/shard_map/ppermute | solution.py:43
  172.9 31.2 %collective-permute-start.24 = (bf16[2,512,512]{2,1,0:T(8,128)(2,1)}, bf16[2,512,512]{2,1,0:T(8,128)(2,1)}, u32[]{:S(2)}, u32[]{:S(2)}) collective-permute-start(bf16[2,512,512]{2,1,0:T(8,128)(2,1)} %collective-permute-done.22.refs_10_), channel_id=1, source_target_pairs={{0,6},{1,7},{2,0},{3,1},{4,2},{5,3},{6,4},{7,5},{8,14},{9,15},{10,... | collective-permute-start | bytes 3145736 | tf_op jit(solution)/shard_map/ppermute | solution.py:43
  181.7 40.0 %collective-permute-start.25 = (bf16[2,512,512]{2,1,0:T(8,128)(2,1)S(1)}, bf16[2,512,512]{2,1,0:T(8,128)(2,1)}, u32[]{:S(2)}, u32[]{:S(2)}) collective-permute-start(bf16[2,512,512]{2,1,0:T(8,128)(2,1)S(1)} %pad_maximum_fusion.1.refs_1_), channel_id=1, source_target_pairs={{0,6},{1,7},{2,0},{3,1},{4,2},{5,3},{6,4},{7,5},{8,14},{9,15},{10,... | collective-permute-start | bytes 3145736 | tf_op jit(solution)/shard_map/ppermute | solution.py:43
  193.3 28.4 %collective-permute-start.26 = (bf16[2,512,512]{2,1,0:T(8,128)(2,1)}, bf16[2,512,512]{2,1,0:T(8,128)(2,1)}, u32[]{:S(2)}, u32[]{:S(2)}) collective-permute-start(bf16[2,512,512]{2,1,0:T(8,128)(2,1)} %collective-permute-done.9.refs_2_), channel_id=1, source_target_pairs={{0,6},{1,7},{2,0},{3,1},{4,2},{5,3},{6,4},{7,5},{8,14},{9,15},{10,... | collective-permute-start | bytes 3145736 | tf_op jit(solution)/shard_map/ppermute | solution.py:43
  193.9 41.6 %collective-permute-start.10 = (bf16[2,512,512]{2,1,0:T(8,128)(2,1)}, bf16[2,512,512]{2,1,0:T(8,128)(2,1)}, u32[]{:S(2)}, u32[]{:S(2)}) collective-permute-start(bf16[2,512,512]{2,1,0:T(8,128)(2,1)} %collective-permute-done.9.refs_2_), channel_id=1, source_target_pairs={{0,2},{1,3},{2,4},{3,5},{4,6},{5,7},{6,0},{7,1},{8,10},{9,11},{10,... | collective-permute-start | bytes 3145736 | tf_op jit(solution)/shard_map/ppermute | solution.py:43
  204.2 31.3 %collective-permute-start.15 = (bf16[2,512,512]{2,1,0:T(8,128)(2,1)}, bf16[2,512,512]{2,1,0:T(8,128)(2,1)}, u32[]{:S(2)}, u32[]{:S(2)}) collective-permute-start(bf16[2,512,512]{2,1,0:T(8,128)(2,1)} %collective-permute-done.14.refs_3_), channel_id=1, source_target_pairs={{0,2},{1,3},{2,4},{3,5},{4,6},{5,7},{6,0},{7,1},{8,10},{9,11},{10,... | collective-permute-start | bytes 3145736 | tf_op jit(solution)/shard_map/ppermute | solution.py:43
  204.2 25.6 %collective-permute-start.27 = (bf16[2,512,512]{2,1,0:T(8,128)(2,1)}, bf16[2,512,512]{2,1,0:T(8,128)(2,1)}, u32[]{:S(2)}, u32[]{:S(2)}) collective-permute-start(bf16[2,512,512]{2,1,0:T(8,128)(2,1)} %collective-permute-done.24.refs_12_), channel_id=1, source_target_pairs={{0,1},{1,0},{2,3},{3,2},{4,5},{5,4},{6,7},{7,6},{8,9},{9,8},{10,11... | collective-permute-start | bytes 3145736 | tf_op jit(solution)/shard_map/ppermute | solution.py:43
  (28 other events, 569.2 us)
where the time goes:
time: 243 us; the launch traced here: 241 us
  waiting for transfers between devices  87.7 us (36%)
  starting transfers between devices  63 us (26%)
  Pallas kernels  40.4 us (17%)
  blocking collectives  29.5 us (12%)
  local copies, waits for them, and re-layouts  13.5 us (6%)
  other arithmetic  5.56 us (2%)
    ppermute x28, waiting for transfers between devices, permute(): return lax.ppermute(array, AXES, pairs)  76.5 us
    ppermute x28, starting transfers between devices, permute(): return lax.ppermute(array, AXES, pairs)  43.2 us
    all_to_all x1, blocking collectives, shards(): lax.all_to_all(attended, TOK_AXES, split_axis=0, concat_axis=0, tiled=True)  29.5 us
    pallas_call x3, Pallas kernels, moment(): pl.pallas_call(lambda *refs: moment_kernel(count, stage, *refs), out_shap...  20.1 us
    all_to_all x1, starting transfers between devices, shards(): lax.all_to_all(narrow.reshape(FSDP, ROWS, 2 * KV + 128), TOK_AXES, split_...  9.4 us
    unnamed x43, local copies, waits for them, and re-layouts  9.2 us
    pallas_call x1, Pallas kernels, mix(): pl.pallas_call(mix_kernel, out_shape=[jax.ShapeDtypeStruct((GT, FW), bf16...  6.64 us
    all_to_all x1, waiting for transfers between devices, shards(): lax.all_to_all(square, TOK_AXES, split_axis=0, concat_axis=0, tiled=True)  6.19 us
  transfers between devices with their start and end apart: 31, of which 13 were waited for; matrix products, arithmetic and copies ran while one was open for 4% of the time, Pallas kernels for 9%

commit v1 on v0

--- a/solution.py
+++ b/solution.py
@@ -21,7 +21,7 @@
 ROWS = GT // FSDP
 QW = KEEP * HEAD
 KV = KVW * HEAD
-STEP = 4
+STEP = 8
 
 epsilon = 1e-05
 
@@ -160,9 +160,8 @@
     ws, refs = refs[:STEP], refs[STEP:]
     scale, h, gain, residual, gained, acc = refs
     j = pl.program_id(0)
-    a = att[:, pl.ds(pl.multiple_of(j * STEP * HEAD, STEP * HEAD), STEP * HEAD)]
     w = jnp.concatenate([r[...] for r in ws], axis=0)
-    part = jnp.dot(a, w, preferred_element_type=f32)
+    part = jnp.dot(att[...], w, preferred_element_type=f32)
 
     @pl.when(j == 0)
     def _():
@@ -189,7 +188,7 @@
             num_scalar_prefetch=1,
             grid=(KEEP // STEP,),
             in_specs=[
-                whole((GT, QW)),
+                pl.BlockSpec((GT, STEP * HEAD), lambda j, kept: (0, j)),
                 *[head(i) for i in range(STEP)],
                 whole((1, FW)),
                 whole((GT, FW)),
@@ -339,7 +338,8 @@
     other = permute(own, other_yl)
     a = [own] + [permute(own, along_first(d)) for d in (1, -1, 2)]
     pieces = {(0, 0, half): jnp.stack(a[2 * half : 2 * half + 2]) for half in range(2)}
-    pieces[1, 0, 0] = jnp.stack([other, permute(a[1], other_yl)])
+    crossed = permute(a[1], other_yl)
+    pieces[1, 0, 0] = jnp.stack([other, crossed])
     pieces[1, 0, 1] = permute(pieces[0, 0, 1], other_yl)
     for e in range(2):
         for half in range(2):

time: 243 us -> 242 us (level)
  no operation moved by 1% of the time
where the time goes in v1:
time: 242 us; the launch traced here: 240 us
  waiting for transfers between devices  88.4 us (37%)
  starting transfers between devices  63 us (26%)
  Pallas kernels  38.5 us (16%)
  blocking collectives  29.5 us (12%)
  local copies, waits for them, and re-layouts  13.5 us (6%)
  other arithmetic  5.56 us (2%)
    ppermute x28, waiting for transfers between devices, permute(): return lax.ppermute(array, AXES, pairs)  76.4 us
    ppermute x28, starting transfers between devices, permute(): return lax.ppermute(array, AXES, pairs)  43.2 us
    all_to_all x1, blocking collectives, shards(): lax.all_to_all(attended, TOK_AXES, split_axis=0, concat_axis=0, tiled=True)  29.5 us
    pallas_call x3, Pallas kernels, moment(): pl.pallas_call(lambda *refs: moment_kernel(count, stage, *refs), out_shap...  20.1 us
    all_to_all x1, starting transfers between devices, shards(): lax.all_to_all(narrow.reshape(FSDP, ROWS, 2 * KV + 128), TOK_AXES, split_...  9.4 us
    unnamed x43, local copies, waits for them, and re-layouts  9.21 us
    all_to_all x1, waiting for transfers between devices, shards(): lax.all_to_all(square, TOK_AXES, split_axis=0, concat_axis=0, tiled=True)  6.19 us
    all_to_all x1, waiting for transfers between devices, shards(): lax.all_to_all(narrow.reshape(FSDP, ROWS, 2 * KV + 128), TOK_AXES, split_...  5.78 us
  transfers between devices with their start and end apart: 31, of which 13 were waited for; matrix products, arithmetic and copies ran while one was open for 4% of the time, Pallas kernels for 9%

profile of v1, /device:TPU:24, one launch (start us, length us, event | category | flops | bytes accessed | tf_op | source)
XLA Modules:
  0.0 239.7 jit_solution(4143407409203415823)
XLA Ops:
  3.1 9.4 %all-to-all-start.1 = ((bf16[32,16,640]{2,1,0:T(8,128)(2,1)}), bf16[32,16,640]{2,1,0:T(8,128)(2,1)S(1)}, u32[]{:S(2)}, u32[]{:S(2)}) async-start(bf16[32,16,640]{2,1,0:T(8,128)(2,1)} %bitcast.47), calls=%async_computation.1 | async-start | bytes 1310720 | tf_op jit(solution)/shard_map/all_to_all | solution.py:300
  13.8 5.1 %shard_map.213 = bf16[512,2048]{1,0:T(8,128)(2,1)} custom-call(s32[16]{0:T(128)} %get-tuple-element.33.kept, bf16[512,512]{1,0:T(8,128)(2,1)} %get-tuple-element.11.hg, bf16[512,4096]{1,0:T(8,128)(2,1)} %refs_7_.2, bf16[512,4096]{1,0:T(8,128)(2,1)} %refs_7_.2, bf16[512,4096]{1,0:T(8,128)(2,1)} %refs_7_.2, bf16[512,4096]{1,0:T(8,128)(2,1)} %refs_7_.2, ...), custom_call_target="tpu_custom_call" | custom-call | tf_op jit(solution)/shard_map/pallas_call | solution.py:108
  18.9 5.8 %all-to-all-done.1.x = bf16[32,16,640]{2,1,0:T(8,128)(2,1)S(1)} async-done(((bf16[32,16,640]{2,1,0:T(8,128)(2,1)}), bf16[32,16,640]{2,1,0:T(8,128)(2,1)S(1)}, u32[]{:S(2)}, u32[]{:S(2)}) %all-to-all-start.1) | async-done | bytes 655392 | tf_op jit(solution)/shard_map/all_to_all | solution.py:300
  24.7 4.9 %all-to-all-start = ((bf16[32,16,2048]{2,1,0:T(8,128)(2,1)}), bf16[32,16,2048]{2,1,0:T(8,128)(2,1)S(1)}, u32[]{:S(2)}, u32[]{:S(2)}) async-start(bf16[32,16,2048]{2,1,0:T(8,128)(2,1)} %bitcast.37), calls=%async_computation | async-start | bytes 4194304 | tf_op jit(solution)/shard_map/all_to_all | solution.py:302
  33.0 3.0 %collective-permute-start.2 = (bf16[16,512]{1,0:T(8,128)(2,1)}, bf16[16,512]{1,0:T(8,128)(2,1)S(1)}, u32[]{:S(2)}, u32[]{:S(2)}) collective-permute-start(bf16[16,512]{1,0:T(8,128)(2,1)} %get-tuple-element.14), channel_id=1, source_target_pairs={{0,4},{1,5},{2,6},{3,7},{4,0},{5,1},{6,2},{7,3},{8,12},{9,13},{10,... | collective-permute-start | bytes 49160 | tf_op jit(solution)/shard_map/ppermute | solution.py:43
  38.0 16.9 %collective-permute-done.2 = bf16[16,512]{1,0:T(8,128)(2,1)S(1)} collective-permute-done((bf16[16,512]{1,0:T(8,128)(2,1)}, bf16[16,512]{1,0:T(8,128)(2,1)S(1)}, u32[]{:S(2)}, u32[]{:S(2)}) %collective-permute-start.2) | collective-permute-done | bytes 16416 | tf_op jit(solution)/shard_map/ppermute | solution.py:43
  55.7 3.6 %collective-permute-start.5 = (bf16[4,16,512]{2,1,0:T(8,128)(2,1)S(1)}, bf16[4,16,512]{2,1,0:T(8,128)(2,1)S(1)}, u32[]{:S(2)}, u32[]{:S(2)}) collective-permute-start(bf16[4,16,512]{2,1,0:T(8,128)(2,1)S(1)} %pad_maximum_fusion.3.kva), channel_id=1, source_target_pairs={{0,16},{1,17},{2,18},{3,19},{4,20},{5,21},{6,22},{7,23},{8,24},{9,... | collective-permute-start | bytes 196616 | tf_op jit(solution)/shard_map/ppermute | solution.py:43
  66.5 3.8 %shard_map.215 = bf16[32,16,2048]{2,1,0:T(8,128)(2,1)} custom-call(bf16[32,16,2048]{2,1,0:T(8,128)(2,1)S(1)} %all-to-all-done.x, f32[16,128]{1,0:T(8,128)} %get-tuple-element.13.inverse, f32[16,128]{1,0:T(8,128)} %pad_maximum_fusion.4.cosine, f32[16,128]{1,0:T(8,128)} %pad_maximum_fusion.5.sine, bf16[4,16,512]{2,1,0:T(8,128)(2,1)} %copy-done.10, ...), custom_call_target="tpu_custom_call" | custom-call | tf_op jit(solution)/shard_map/pallas_call | solution.py:325
  70.3 29.5 %all_to_all.20 = bf16[32,16,2048]{2,1,0:T(8,128)(2,1)} all-to-all(bf16[32,16,2048]{2,1,0:T(8,128)(2,1)} %shard_map.215), channel_id=1, replica_groups=mesh['yh'=2,'core'=2,'z'=4,'x'=4,'yl'=2] {'yl','z','x'}, dimensions={0} | all-to-all | bytes 4194304 | tf_op jit(solution)/shard_map/all_to_all | solution.py:329
  99.8 5.4 %shard_map.216 = (bf16[512,512]{1,0:T(8,128)(2,1)}, bf16[512,512]{1,0:T(8,128)(2,1)}) custom-call(s32[16]{0:T(128)} %get-tuple-element.33.kept, bf16[512,2048]{1,0:T(8,128)(2,1)} %bitcast.38, bf16[4096,512]{1,0:T(8,128)(2,1)} %refs_7_.3, bf16[4096,512]{1,0:T(8,128)(2,1)} %refs_7_.3, bf16[4096,512]{1,0:T(8,128)(2,1)} %refs_7_.3, bf16[4096,512]{1,0:T(8,128)(2,1)} %refs_7_.3, ...), custom_call_target="tpu_custom_call" | custom-call | tf_op jit(solution)/shard_map/pallas_call | solution.py:184
  105.2 3.7 %collective-permute-start.6 = (bf16[512,512]{1,0:T(8,128)(2,1)}, bf16[512,512]{1,0:T(8,128)(2,1)S(1)}, u32[]{:S(2)}, u32[]{:S(2)}) collective-permute-start(bf16[512,512]{1,0:T(8,128)(2,1)} %get-tuple-element.15), channel_id=1, source_target_pairs={{0,0},{1,1},{2,2},{3,3},{4,4},{5,5},{6,6},{7,7},{8,40},{9,41},{10,... | collective-permute-start | bytes 1572872 | tf_op jit(solution)/shard_map/ppermute | solution.py:43
  110.7 5.5 %all-to-all-start.3 = ((f32[32,1,512]{2,1,0:T(1,128)}), f32[32,1,512]{2,1,0:T(1,128)S(1)}, u32[]{:S(2)}, u32[]{:S(2)}) async-start(f32[32,1,512]{2,1,0:T(1,128)} %broadcast_in_dim.38), calls=%async_computation.3 | async-start | bytes 131072 | tf_op jit(solution)/shard_map/all_to_all | solution.py:335
  117.6 6.2 %all-to-all-done.3 = f32[32,1,512]{2,1,0:T(1,128)S(1)} async-done(((f32[32,1,512]{2,1,0:T(1,128)}), f32[32,1,512]{2,1,0:T(1,128)S(1)}, u32[]{:S(2)}, u32[]{:S(2)}) %all-to-all-start.3) | async-done | bytes 65568 | tf_op jit(solution)/shard_map/all_to_all | solution.py:335
  131.8 8.1 %collective-permute-done.12 = bf16[512,512]{1,0:T(8,128)(2,1)S(1)} collective-permute-done((bf16[512,512]{1,0:T(8,128)(2,1)S(1)}, bf16[512,512]{1,0:T(8,128)(2,1)S(1)}, u32[]{:S(2)}, u32[]{:S(2)}) %collective-permute-start.12) | collective-permute-done | bytes 524320 | tf_op jit(solution)/shard_map/ppermute | solution.py:43
  144.8 5.4 %collective-permute-start.22 = (bf16[2,512,512]{2,1,0:T(8,128)(2,1)S(1)}, bf16[2,512,512]{2,1,0:T(8,128)(2,1)}, u32[]{:S(2)}, u32[]{:S(2)}) collective-permute-start(bf16[2,512,512]{2,1,0:T(8,128)(2,1)S(1)} %pad_maximum_fusion.refs_6_), channel_id=1, source_target_pairs={{0,6},{1,7},{2,0},{3,1},{4,2},{5,3},{6,4},{7,5},{8,14},{9,15},{10,... | collective-permute-start | bytes 3145736 | tf_op jit(solution)/shard_map/ppermute | solution.py:43
  150.2 5.7 %collective-permute-done.11 = bf16[512,512]{1,0:T(8,128)(2,1)S(1)} collective-permute-done((bf16[512,512]{1,0:T(8,128)(2,1)S(1)}, bf16[512,512]{1,0:T(8,128)(2,1)S(1)}, u32[]{:S(2)}, u32[]{:S(2)}) %collective-permute-start.11) | collective-permute-done | bytes 524320 | tf_op jit(solution)/shard_map/ppermute | solution.py:43
  155.9 7.5 %collective-permute-done.13 = bf16[512,512]{1,0:T(8,128)(2,1)S(1)} collective-permute-done((bf16[512,512]{1,0:T(8,128)(2,1)S(1)}, bf16[512,512]{1,0:T(8,128)(2,1)S(1)}, u32[]{:S(2)}, u32[]{:S(2)}) %collective-permute-start.13) | collective-permute-done | bytes 524320 | tf_op jit(solution)/shard_map/ppermute | solution.py:43
  174.1 6.3 %collective-permute-done.20.refs_8_ = bf16[2,512,512]{2,1,0:T(8,128)(2,1)} collective-permute-done((bf16[2,512,512]{2,1,0:T(8,128)(2,1)S(1)}, bf16[2,512,512]{2,1,0:T(8,128)(2,1)}, u32[]{:S(2)}, u32[]{:S(2)}) %collective-permute-start.20) | collective-permute-done | bytes 1048608 | tf_op jit(solution)/shard_map/ppermute | solution.py:43
  180.5 11.6 %collective-permute-done.9.refs_2_ = bf16[2,512,512]{2,1,0:T(8,128)(2,1)} collective-permute-done((bf16[2,512,512]{2,1,0:T(8,128)(2,1)S(1)}, bf16[2,512,512]{2,1,0:T(8,128)(2,1)}, u32[]{:S(2)}, u32[]{:S(2)}) %collective-permute-start.9) | collective-permute-done | bytes 1048608 | tf_op jit(solution)/shard_map/ppermute | solution.py:43
  194.1 8.9 %collective-permute-done.23.refs_11_ = bf16[2,512,512]{2,1,0:T(8,128)(2,1)} collective-permute-done((bf16[2,512,512]{2,1,0:T(8,128)(2,1)}, bf16[2,512,512]{2,1,0:T(8,128)(2,1)}, u32[]{:S(2)}, u32[]{:S(2)}) %collective-permute-start.23) | collective-permute-done | bytes 1048608 | tf_op jit(solution)/shard_map/ppermute | solution.py:43
  211.2 9.2 %shard_map.217 = (bf16[4,512,512]{2,1,0:T(8,128)(2,1)S(1)}, f32[512,4096]{1,0:T(8,128)}) custom-call(s32[17,2]{1,0:T(8,128)S(1)} %concatenate.18.refs_0_, bf16[512,512]{1,0:T(8,128)(2,1)S(1)} %copy-done.1, bf16[512,512]{1,0:T(8,128)(2,1)S(1)} %copy-done.5, bf16[512,512]{1,0:T(8,128)(2,1)S(1)} %copy-done.7, bf16[512,512]{1,0:T(8,128)(2,1)S(1)} %copy-done.9, ...), custom_call_target="tpu_custom_call" | custom-call | tf_op jit(solution)/shard_map/pallas_call | solution.py:264
  220.5 8.1 %collective-permute-done.27.refs_6_ = bf16[2,512,512]{2,1,0:T(8,128)(2,1)} collective-permute-done((bf16[2,512,512]{2,1,0:T(8,128)(2,1)}, bf16[2,512,512]{2,1,0:T(8,128)(2,1)}, u32[]{:S(2)}, u32[]{:S(2)}) %collective-permute-start.27) | collective-permute-done | bytes 1048608 | tf_op jit(solution)/shard_map/ppermute | solution.py:43
  228.6 5.6 %shard_map.218.refs_4_ = f32[4,512,512]{2,1,0:T(8,128)S(1)} custom-call(s32[13,2]{1,0:T(8,128)S(1)} %concatenate.19.refs_0_, bf16[2,512,512]{2,1,0:T(8,128)(2,1)S(1)} %pad_maximum_fusion.1.refs_1_, bf16[2,512,512]{2,1,0:T(8,128)(2,1)} %collective-permute-done.9.refs_2_, bf16[2,512,512]{2,1,0:T(8,128)(2,1)} %collective-permute-done.14.refs_3_, ...), custom_call_target="tpu_custom_call" | custom-call | tf_op jit(solution)/shard_map/pallas_call | solution.py:264
  234.2 5.3 %shard_map.219 = (f32[4,512,512]{2,1,0:T(8,128)S(1)}, f32[512,4096]{1,0:T(8,128)}) custom-call(s32[5,2]{1,0:T(8,128)S(1)} %concatenate.15.refs_0_, bf16[2,512,512]{2,1,0:T(8,128)(2,1)} %collective-permute-done.10.refs_1_, bf16[2,512,512]{2,1,0:T(8,128)(2,1)} %collective-permute-done.15.refs_2_, ...), custom_call_target="tpu_custom_call", output_to_operand_aliasing={{0}: (4, {}), {1}: (5, {})} | custom-call | tf_op jit(solution)/shard_map/pallas_call | solution.py:264
  (136 shorter events, 54.2 us)
Async XLA Ops:
  3.1 21.6 %all-to-all-start.1 = ((bf16[32,16,640]{2,1,0:T(8,128)(2,1)}), bf16[32,16,640]{2,1,0:T(8,128)(2,1)S(1)}, u32[]{:S(2)}, u32[]{:S(2)}) async-start(bf16[32,16,640]{2,1,0:T(8,128)(2,1)} %bitcast.47), calls=%async_computation.1 | async-start | bytes 1310720 | tf_op jit(solution)/shard_map/all_to_all | solution.py:300
  24.7 41.2 %all-to-all-start = ((bf16[32,16,2048]{2,1,0:T(8,128)(2,1)}), bf16[32,16,2048]{2,1,0:T(8,128)(2,1)S(1)}, u32[]{:S(2)}, u32[]{:S(2)}) async-start(bf16[32,16,2048]{2,1,0:T(8,128)(2,1)} %bitcast.37), calls=%async_computation | async-start | bytes 4194304 | tf_op jit(solution)/shard_map/all_to_all | solution.py:302
  33.0 21.9 %collective-permute-start.2 = (bf16[16,512]{1,0:T(8,128)(2,1)}, bf16[16,512]{1,0:T(8,128)(2,1)S(1)}, u32[]{:S(2)}, u32[]{:S(2)}) collective-permute-start(bf16[16,512]{1,0:T(8,128)(2,1)} %get-tuple-element.14), channel_id=1, source_target_pairs={{0,4},{1,5},{2,6},{3,7},{4,0},{5,1},{6,2},{7,3},{8,12},{9,13},{10,... | collective-permute-start | bytes 49160 | tf_op jit(solution)/shard_map/ppermute | solution.py:43
  35.9 19.0 %collective-permute-start.1 = (bf16[16,512]{1,0:T(8,128)(2,1)}, bf16[16,512]{1,0:T(8,128)(2,1)S(1)}, u32[]{:S(2)}, u32[]{:S(2)}) collective-permute-start(bf16[16,512]{1,0:T(8,128)(2,1)} %get-tuple-element.14), channel_id=1, source_target_pairs={{0,6},{1,7},{2,0},{3,1},{4,2},{5,3},{6,4},{7,5},{8,14},{9,15},{10,... | collective-permute-start | bytes 49160 | tf_op jit(solution)/shard_map/ppermute | solution.py:43
  37.1 17.8 %collective-permute-start = (bf16[16,512]{1,0:T(8,128)(2,1)}, bf16[16,512]{1,0:T(8,128)(2,1)S(1)}, u32[]{:S(2)}, u32[]{:S(2)}) collective-permute-start(bf16[16,512]{1,0:T(8,128)(2,1)} %get-tuple-element.14), channel_id=1, source_target_pairs={{0,2},{1,3},{2,4},{3,5},{4,6},{5,7},{6,0},{7,1},{8,10},{9,11},{10,... | collective-permute-start | bytes 49160 | tf_op jit(solution)/shard_map/ppermute | solution.py:43
  105.2 18.7 %collective-permute-start.6 = (bf16[512,512]{1,0:T(8,128)(2,1)}, bf16[512,512]{1,0:T(8,128)(2,1)S(1)}, u32[]{:S(2)}, u32[]{:S(2)}) collective-permute-start(bf16[512,512]{1,0:T(8,128)(2,1)} %get-tuple-element.15), channel_id=1, source_target_pairs={{0,0},{1,1},{2,2},{3,3},{4,4},{5,5},{6,6},{7,7},{8,40},{9,41},{10,... | collective-permute-start | bytes 1572872 | tf_op jit(solution)/shard_map/ppermute | solution.py:43
  123.8 16.1 %collective-permute-start.12 = (bf16[512,512]{1,0:T(8,128)(2,1)S(1)}, bf16[512,512]{1,0:T(8,128)(2,1)S(1)}, u32[]{:S(2)}, u32[]{:S(2)}) collective-permute-start(bf16[512,512]{1,0:T(8,128)(2,1)S(1)} %collective-permute-done.6), channel_id=1, source_target_pairs={{0,8},{1,9},{2,10},{3,11},{4,12},{5,13},{6,14},{7,15},{8,16},{9,17... | collective-permute-start | bytes 1572872 | tf_op jit(solution)/shard_map/ppermute | solution.py:43
  124.2 17.5 %collective-permute-start.8 = (bf16[512,512]{1,0:T(8,128)(2,1)S(1)}, bf16[512,512]{1,0:T(8,128)(2,1)S(1)}, u32[]{:S(2)}, u32[]{:S(2)}) collective-permute-start(bf16[512,512]{1,0:T(8,128)(2,1)S(1)} %collective-permute-done.6), channel_id=1, source_target_pairs={{0,16},{1,17},{2,18},{3,19},{4,20},{5,21},{6,22},{7,23},{8,24},{9,... | collective-permute-start | bytes 1572872 | tf_op jit(solution)/shard_map/ppermute | solution.py:43
  128.4 16.4 %collective-permute-start.16 = (bf16[512,512]{1,0:T(8,128)(2,1)S(1)}, bf16[512,512]{1,0:T(8,128)(2,1)S(1)}, u32[]{:S(2)}, u32[]{:S(2)}) collective-permute-start(bf16[512,512]{1,0:T(8,128)(2,1)S(1)} %fusion.refs_1_), channel_id=1, source_target_pairs={{0,64},{1,65},{2,66},{3,67},{4,68},{5,69},{6,70},{7,71},{8,72},{9,... | collective-permute-start | bytes 1572872 | tf_op jit(solution)/shard_map/ppermute | solution.py:43
  131.4 24.5 %collective-permute-start.11 = (bf16[512,512]{1,0:T(8,128)(2,1)S(1)}, bf16[512,512]{1,0:T(8,128)(2,1)S(1)}, u32[]{:S(2)}, u32[]{:S(2)}) collective-permute-start(bf16[512,512]{1,0:T(8,128)(2,1)S(1)} %collective-permute-done.6), channel_id=1, source_target_pairs={{0,1},{1,0},{2,3},{3,2},{4,5},{5,4},{6,7},{7,6},{8,9},{9,8},{10,11... | collective-permute-start | bytes 1572872 | tf_op jit(solution)/shard_map/ppermute | solution.py:43
  140.0 28.5 %collective-permute-start.21 = (bf16[2,512,512]{2,1,0:T(8,128)(2,1)S(1)}, bf16[2,512,512]{2,1,0:T(8,128)(2,1)S(1)}, u32[]{:S(2)}, u32[]{:S(2)}) collective-permute-start(bf16[2,512,512]{2,1,0:T(8,128)(2,1)S(1)} %pad_maximum_fusion.2.refs_5_), channel_id=1, source_target_pairs={{0,6},{1,7},{2,0},{3,1},{4,2},{5,3},{6,4},{7,5},{8,14},{9,15},{10,... | collective-permute-start | bytes 3145736 | tf_op jit(solution)/shard_map/ppermute | solution.py:43
  141.7 29.0 %collective-permute-start.19 = (bf16[2,512,512]{2,1,0:T(8,128)(2,1)S(1)}, bf16[2,512,512]{2,1,0:T(8,128)(2,1)}, u32[]{:S(2)}, u32[]{:S(2)}) collective-permute-start(bf16[2,512,512]{2,1,0:T(8,128)(2,1)S(1)} %pad_maximum_fusion.2.refs_5_), channel_id=1, source_target_pairs={{0,2},{1,3},{2,4},{3,5},{4,6},{5,7},{6,0},{7,1},{8,10},{9,11},{10,... | collective-permute-start | bytes 3145736 | tf_op jit(solution)/shard_map/ppermute | solution.py:43
  142.1 21.3 %collective-permute-start.13 = (bf16[512,512]{1,0:T(8,128)(2,1)S(1)}, bf16[512,512]{1,0:T(8,128)(2,1)S(1)}, u32[]{:S(2)}, u32[]{:S(2)}) collective-permute-start(bf16[512,512]{1,0:T(8,128)(2,1)S(1)} %collective-permute-done.12), channel_id=1, source_target_pairs={{0,1},{1,0},{2,3},{3,2},{4,5},{5,4},{6,7},{7,6},{8,9},{9,8},{10,11... | collective-permute-start | bytes 1572872 | tf_op jit(solution)/shard_map/ppermute | solution.py:43
  144.8 26.9 %collective-permute-start.22 = (bf16[2,512,512]{2,1,0:T(8,128)(2,1)S(1)}, bf16[2,512,512]{2,1,0:T(8,128)(2,1)}, u32[]{:S(2)}, u32[]{:S(2)}) collective-permute-start(bf16[2,512,512]{2,1,0:T(8,128)(2,1)S(1)} %pad_maximum_fusion.refs_6_), channel_id=1, source_target_pairs={{0,6},{1,7},{2,0},{3,1},{4,2},{5,3},{6,4},{7,5},{8,14},{9,15},{10,... | collective-permute-start | bytes 3145736 | tf_op jit(solution)/shard_map/ppermute | solution.py:43
  164.3 16.1 %collective-permute-start.20 = (bf16[2,512,512]{2,1,0:T(8,128)(2,1)S(1)}, bf16[2,512,512]{2,1,0:T(8,128)(2,1)}, u32[]{:S(2)}, u32[]{:S(2)}) collective-permute-start(bf16[2,512,512]{2,1,0:T(8,128)(2,1)S(1)} %pad_maximum_fusion.refs_6_), channel_id=1, source_target_pairs={{0,2},{1,3},{2,4},{3,5},{4,6},{5,7},{6,0},{7,1},{8,10},{9,11},{10,... | collective-permute-start | bytes 3145736 | tf_op jit(solution)/shard_map/ppermute | solution.py:43
  166.1 25.9 %collective-permute-start.9 = (bf16[2,512,512]{2,1,0:T(8,128)(2,1)S(1)}, bf16[2,512,512]{2,1,0:T(8,128)(2,1)}, u32[]{:S(2)}, u32[]{:S(2)}) collective-permute-start(bf16[2,512,512]{2,1,0:T(8,128)(2,1)S(1)} %pad_maximum_fusion.refs_6_), channel_id=1, source_target_pairs={{0,1},{1,0},{2,3},{3,2},{4,5},{5,4},{6,7},{7,6},{8,9},{9,8},{10,11... | collective-permute-start | bytes 3145736 | tf_op jit(solution)/shard_map/ppermute | solution.py:43
  169.4 23.2 %collective-permute-start.14 = (bf16[2,512,512]{2,1,0:T(8,128)(2,1)S(1)}, bf16[2,512,512]{2,1,0:T(8,128)(2,1)}, u32[]{:S(2)}, u32[]{:S(2)}) collective-permute-start(bf16[2,512,512]{2,1,0:T(8,128)(2,1)S(1)} %pad_maximum_fusion.1.refs_1_), channel_id=1, source_target_pairs={{0,2},{1,3},{2,4},{3,5},{4,6},{5,7},{6,0},{7,1},{8,10},{9,11},{10,... | collective-permute-start | bytes 3145736 | tf_op jit(solution)/shard_map/ppermute | solution.py:43
  170.7 32.2 %collective-permute-start.23 = (bf16[2,512,512]{2,1,0:T(8,128)(2,1)}, bf16[2,512,512]{2,1,0:T(8,128)(2,1)}, u32[]{:S(2)}, u32[]{:S(2)}) collective-permute-start(bf16[2,512,512]{2,1,0:T(8,128)(2,1)} %collective-permute-done.19.refs_7_), channel_id=1, source_target_pairs={{0,2},{1,3},{2,4},{3,5},{4,6},{5,7},{6,0},{7,1},{8,10},{9,11},{10,... | collective-permute-start | bytes 3145736 | tf_op jit(solution)/shard_map/ppermute | solution.py:43
  171.7 31.2 %collective-permute-start.24 = (bf16[2,512,512]{2,1,0:T(8,128)(2,1)}, bf16[2,512,512]{2,1,0:T(8,128)(2,1)}, u32[]{:S(2)}, u32[]{:S(2)}) collective-permute-start(bf16[2,512,512]{2,1,0:T(8,128)(2,1)} %collective-permute-done.22.refs_10_), channel_id=1, source_target_pairs={{0,6},{1,7},{2,0},{3,1},{4,2},{5,3},{6,4},{7,5},{8,14},{9,15},{10,... | collective-permute-start | bytes 3145736 | tf_op jit(solution)/shard_map/ppermute | solution.py:43
  180.5 40.0 %collective-permute-start.25 = (bf16[2,512,512]{2,1,0:T(8,128)(2,1)S(1)}, bf16[2,512,512]{2,1,0:T(8,128)(2,1)}, u32[]{:S(2)}, u32[]{:S(2)}) collective-permute-start(bf16[2,512,512]{2,1,0:T(8,128)(2,1)S(1)} %pad_maximum_fusion.1.refs_1_), channel_id=1, source_target_pairs={{0,6},{1,7},{2,0},{3,1},{4,2},{5,3},{6,4},{7,5},{8,14},{9,15},{10,... | collective-permute-start | bytes 3145736 | tf_op jit(solution)/shard_map/ppermute | solution.py:43
  192.0 28.4 %collective-permute-start.26 = (bf16[2,512,512]{2,1,0:T(8,128)(2,1)}, bf16[2,512,512]{2,1,0:T(8,128)(2,1)}, u32[]{:S(2)}, u32[]{:S(2)}) collective-permute-start(bf16[2,512,512]{2,1,0:T(8,128)(2,1)} %collective-permute-done.9.refs_2_), channel_id=1, source_target_pairs={{0,6},{1,7},{2,0},{3,1},{4,2},{5,3},{6,4},{7,5},{8,14},{9,15},{10,... | collective-permute-start | bytes 3145736 | tf_op jit(solution)/shard_map/ppermute | solution.py:43
  192.6 41.6 %collective-permute-start.10 = (bf16[2,512,512]{2,1,0:T(8,128)(2,1)}, bf16[2,512,512]{2,1,0:T(8,128)(2,1)}, u32[]{:S(2)}, u32[]{:S(2)}) collective-permute-start(bf16[2,512,512]{2,1,0:T(8,128)(2,1)} %collective-permute-done.9.refs_2_), channel_id=1, source_target_pairs={{0,2},{1,3},{2,4},{3,5},{4,6},{5,7},{6,0},{7,1},{8,10},{9,11},{10,... | collective-permute-start | bytes 3145736 | tf_op jit(solution)/shard_map/ppermute | solution.py:43
  202.9 31.3 %collective-permute-start.15 = (bf16[2,512,512]{2,1,0:T(8,128)(2,1)}, bf16[2,512,512]{2,1,0:T(8,128)(2,1)}, u32[]{:S(2)}, u32[]{:S(2)}) collective-permute-start(bf16[2,512,512]{2,1,0:T(8,128)(2,1)} %collective-permute-done.14.refs_3_), channel_id=1, source_target_pairs={{0,2},{1,3},{2,4},{3,5},{4,6},{5,7},{6,0},{7,1},{8,10},{9,11},{10,... | collective-permute-start | bytes 3145736 | tf_op jit(solution)/shard_map/ppermute | solution.py:43
  202.9 25.6 %collective-permute-start.27 = (bf16[2,512,512]{2,1,0:T(8,128)(2,1)}, bf16[2,512,512]{2,1,0:T(8,128)(2,1)}, u32[]{:S(2)}, u32[]{:S(2)}) collective-permute-start(bf16[2,512,512]{2,1,0:T(8,128)(2,1)} %collective-permute-done.24.refs_12_), channel_id=1, source_target_pairs={{0,1},{1,0},{2,3},{3,2},{4,5},{5,4},{6,7},{7,6},{8,9},{9,8},{10,11... | collective-permute-start | bytes 3145736 | tf_op jit(solution)/shard_map/ppermute | solution.py:43
  (28 other events, 569.9 us)
